TPU v7x, 32 devices: a whole 2x2x4 slice. The times are simulated.
32 devices in a mesh: dp: 16 (over z, x, core), mp: 2 (over y).
Axes of the slice: x: 2, y: 2, z: 4, core: 2. Of those that a mesh axis runs over, the one named last changes fastest.
Arguments:
- tokens: bfloat16 [64, 512, 768], P('dp', 'mp'), may hold values from -6 to 6
- lengths: int32 [64], P('dp'), may hold values from 128 to 512, as said below
- out_grad: bfloat16 [64, 512, 768], P('dp', 'mp'), may hold values from -6 to 6
- ln1_gain: float32 [768], replicated, may hold values from 0.25 to 1.75
- ln1_shift: float32 [768], replicated, may hold values from -1.75 to 1.75
- w_query: bfloat16 [768, 768], P(None, 'mp'), may hold values from -0.21875 to 0.21875
- b_query: float32 [768], P('mp'), may hold values from -3 to 3
- w_key: bfloat16 [768, 768], P(None, 'mp'), may hold values from -0.21875 to 0.21875
- w_value: bfloat16 [768, 768], P(None, 'mp'), may hold values from -0.21875 to 0.21875
- b_value: float32 [768], P('mp'), may hold values from -3 to 3
- w_out: bfloat16 [768, 768], P('mp'), may hold values from -1.75 to 1.75
- b_out: float32 [768], replicated, may hold values from -1.75 to 1.75
- ln2_gain: float32 [768], replicated, may hold values from 0.25 to 1.75
- ln2_shift: float32 [768], replicated, may hold values from -1.75 to 1.75
- w_up: bfloat16 [768, 3072], P(None, 'mp'), may hold values from -0.21875 to 0.21875
- b_up: float32 [3072], P('mp'), may hold values from -3 to 3
- w_down: bfloat16 [3072, 768], P('mp'), may hold values from -0.109375 to 0.109375
- b_down: float32 [768], replicated, may hold values from -1.75 to 1.75
Outputs:
- block_out: bfloat16 [64, 512, 768], P('dp', 'mp')
- input_grad: float32 [64, 512, 768], P('dp', 'mp')
- grad_ln1_gain: float32 [768], replicated
- grad_ln1_shift: float32 [768], replicated
- grad_w_query: float32 [768, 768], P(None, 'mp')
- grad_b_query: float32 [768], P('mp')
- grad_w_key: float32 [768, 768], P(None, 'mp')
- grad_w_value: float32 [768, 768], P(None, 'mp')
- grad_b_value: float32 [768], P('mp')
- grad_w_out: float32 [768, 768], P('mp')
- grad_b_out: float32 [768], replicated
- grad_ln2_gain: float32 [768], replicated
- grad_ln2_shift: float32 [768], replicated
- grad_w_up: float32 [768, 3072], P(None, 'mp')
- grad_b_up: float32 [3072], P('mp')
- grad_w_down: float32 [3072, 768], P('mp')
- grad_b_down: float32 [768], replicated
Inputs may be any that keep to these rules, and one draw needn't show every extreme that they name: lengths of the rows; some row has 512 and some row a quarter of 512.
All inputs are finite; a program needn't handle non-finite values.
Results may differ from a plain program's by a relative error of at most 0.013.
The roundings to bfloat16 on the way count: a program that leaves them out, or rounds other values in their place, can miss the bound.
Values may be sent and summed in bfloat16 or wider, within the bound.
No kernel may reach another device: no remote copies, remote signals or barrier semaphores. Data moves between devices by JAX's collectives and lax.ppermute only.
A program may use at most 192 MiB of HBM per device.

v0:
```python
import math
import jax
import jax.numpy as jnp
from jax import lax
from jax.sharding import PartitionSpec as P

HEAD_DIM = 64
SEQ = 512
MB = 4
ROWS_MB = 1
epsilon = 1e-12
masked_fill = -1000000000.0


def layer_norm(values, gain_vec, offset):
    average = jnp.mean(values, axis=-1, keepdims=True)
    centred = values - average
    inv_std = lax.rsqrt(jnp.mean(centred * centred, axis=-1, keepdims=True) + epsilon)
    unit_part = centred * inv_std
    return (unit_part * gain_vec + offset, unit_part, inv_std)


def norm_back(upstream, unit_part, inv_std, gain_vec):
    scaled = upstream * gain_vec
    return inv_std * (
        scaled
        - jnp.mean(scaled, axis=-1, keepdims=True)
        - unit_part * jnp.mean(scaled * unit_part, axis=-1, keepdims=True)
    )


def gelu_slope(values):
    normal_cdf = 0.5 * (1.0 + lax.erf(values * (1.0 / math.sqrt(2.0))))
    return normal_cdf + values * jnp.exp(-0.5 * values * values) * (1.0 / math.sqrt(2.0 * math.pi))


def product(pattern, left_side, right_side):
    return jnp.einsum(pattern, left_side, right_side, preferred_element_type=jnp.float32)


def token_sum(values):
    return jnp.sum(values, axis=(0, 1))


def masked_scores(query_low, keys_low, key_valid, score_scale):
    raw_scores = product("bqhd,bkhd->bhqk", query_low, keys_low) * score_scale
    return jnp.where(key_valid, raw_scores, masked_fill)


def on_device(
    tokens,
    lengths,
    out_grad,
    ln1_gain,
    ln1_shift,
    w_query,
    b_query,
    w_key,
    w_value,
    b_value,
    w_out,
    b_out,
    ln2_gain,
    ln2_shift,
    w_up,
    b_up,
    w_down,
    b_down,
):
    heads_here = w_query.shape[1] // HEAD_DIM
    score_scale = 1.0 / math.sqrt(HEAD_DIM)
    positions = jnp.arange(SEQ, dtype=jnp.int32)
    sum_w_query = jnp.zeros(w_query.shape, jnp.float32)
    sum_b_query = jnp.zeros(b_query.shape, jnp.float32)
    sum_w_key = jnp.zeros(w_key.shape, jnp.float32)
    sum_w_value = jnp.zeros(w_value.shape, jnp.float32)
    sum_b_value = jnp.zeros(b_value.shape, jnp.float32)
    sum_w_out = jnp.zeros(w_out.shape, jnp.float32)
    sum_w_up = jnp.zeros(w_up.shape, jnp.float32)
    sum_b_up = jnp.zeros(b_up.shape, jnp.float32)
    sum_w_down = jnp.zeros(w_down.shape, jnp.float32)
    sum_ln1_gain = jnp.zeros(ln1_gain.shape, jnp.float32)
    sum_ln1_shift = jnp.zeros(ln1_shift.shape, jnp.float32)
    sum_ln2_gain = jnp.zeros(ln2_gain.shape, jnp.float32)
    sum_ln2_shift = jnp.zeros(ln2_shift.shape, jnp.float32)
    sum_b_out = jnp.zeros(b_out.shape, jnp.float32)
    sum_b_down = jnp.zeros(b_down.shape, jnp.float32)
    outputs = []
    input_grads = []
    for micro_idx in range(MB):
        row_start = micro_idx * ROWS_MB
        inputs = tokens[row_start : row_start + ROWS_MB].astype(jnp.float32)
        row_lengths = lengths[row_start : row_start + ROWS_MB]
        upstream = out_grad[row_start : row_start + ROWS_MB]
        normed_in, unit_in, inv_in = layer_norm(inputs, ln1_gain, ln1_shift)
        full_in = lax.all_gather(normed_in.astype(jnp.bfloat16), "mp", axis=1, tiled=True)
        rows_mb = full_in.shape[0]
        query_low = (
            (product("bsd,de->bse", full_in, w_query) + b_query)
            .astype(jnp.bfloat16)
            .reshape(rows_mb, SEQ, heads_here, HEAD_DIM)
        )
        keys_low = (
            product("bsd,de->bse", full_in, w_key)
            .astype(jnp.bfloat16)
            .reshape(rows_mb, SEQ, heads_here, HEAD_DIM)
        )
        values_low = (
            (product("bsd,de->bse", full_in, w_value) + b_value)
            .astype(jnp.bfloat16)
            .reshape(rows_mb, SEQ, heads_here, HEAD_DIM)
        )
        key_valid = (positions[None, :] < row_lengths[:, None])[:, None, None, :]
        scores = masked_scores(query_low, keys_low, key_valid, score_scale)
        row_max = jnp.max(scores, axis=-1, keepdims=True)
        log_total = row_max + jnp.log(jnp.sum(jnp.exp(scores - row_max), axis=-1, keepdims=True))
        prob_low = jnp.exp(scores - log_total).astype(jnp.bfloat16)
        mixed_low = (
            product("bhqk,bkhd->bqhd", prob_low, values_low)
            .reshape(rows_mb, SEQ, heads_here * HEAD_DIM)
            .astype(jnp.bfloat16)
        )
        attended = lax.psum_scatter(
            product("bse,ed->bsd", mixed_low, w_out), "mp", scatter_dimension=1, tiled=True
        )
        residual = inputs + attended + b_out
        normed_mid, unit_mid, inv_mid = layer_norm(residual, ln2_gain, ln2_shift)
        full_mid = lax.all_gather(normed_mid.astype(jnp.bfloat16), "mp", axis=1, tiled=True)
        hidden = product("bsd,df->bsf", full_mid, w_up) + b_up
        active = jax.nn.gelu(hidden, approximate=False).astype(jnp.bfloat16)
        branch = lax.psum_scatter(
            product("bsf,fd->bsd", active, w_down).astype(jnp.bfloat16),
            "mp",
            scatter_dimension=1,
            tiled=True,
        ).astype(jnp.float32)
        outputs.append((residual + branch + b_down).astype(jnp.bfloat16))
        grad_full = lax.all_gather(upstream, "mp", axis=1, tiled=True)
        upstream_f = upstream.astype(jnp.float32)
        sum_w_down = sum_w_down + product("bsf,bsd->fd", active, grad_full)
        sum_b_down = sum_b_down + token_sum(upstream_f)
        grad_hidden = (product("bsd,fd->bsf", grad_full, w_down) * gelu_slope(hidden)).astype(
            jnp.bfloat16
        )
        sum_w_up = sum_w_up + product("bsd,bsf->df", full_mid, grad_hidden)
        sum_b_up = sum_b_up + token_sum(grad_hidden.astype(jnp.float32))
        grad_norm_mid = lax.psum_scatter(
            product("bsf,df->bsd", grad_hidden, w_up), "mp", scatter_dimension=1, tiled=True
        )
        sum_ln2_gain = sum_ln2_gain + token_sum(grad_norm_mid * unit_mid)
        sum_ln2_shift = sum_ln2_shift + token_sum(grad_norm_mid)
        grad_residual = upstream_f + norm_back(grad_norm_mid, unit_mid, inv_mid, ln2_gain)
        sum_b_out = sum_b_out + token_sum(grad_residual)
        grad_attn = lax.all_gather(grad_residual.astype(jnp.bfloat16), "mp", axis=1, tiled=True)
        sum_w_out = sum_w_out + product("bse,bsd->ed", mixed_low, grad_attn)
        grad_mixed = (
            product("bsd,ed->bse", grad_attn, w_out)
            .astype(jnp.bfloat16)
            .reshape(rows_mb, SEQ, heads_here, HEAD_DIM)
        )
        grad_probs = product("bqhd,bkhd->bhqk", grad_mixed, values_low)
        probs_full = jnp.exp(masked_scores(query_low, keys_low, key_valid, score_scale) - log_total)
        row_delta = jnp.sum(probs_full * grad_probs, axis=-1, keepdims=True)
        grad_scores = (probs_full * (grad_probs - row_delta)).astype(jnp.bfloat16)
        grad_query = (
            (product("bhqk,bkhd->bqhd", grad_scores, keys_low) * score_scale)
            .astype(jnp.bfloat16)
            .reshape(rows_mb, SEQ, heads_here * HEAD_DIM)
        )
        grad_keys = (
            (product("bhqk,bqhd->bkhd", grad_scores, query_low) * score_scale)
            .astype(jnp.bfloat16)
            .reshape(rows_mb, SEQ, heads_here * HEAD_DIM)
        )
        grad_values = (
            product("bhqk,bqhd->bkhd", prob_low, grad_mixed)
            .astype(jnp.bfloat16)
            .reshape(rows_mb, SEQ, heads_here * HEAD_DIM)
        )
        sum_w_query = sum_w_query + product("bsd,bse->de", full_in, grad_query)
        sum_b_query = sum_b_query + token_sum(grad_query.astype(jnp.float32))
        sum_w_key = sum_w_key + product("bsd,bse->de", full_in, grad_keys)
        sum_w_value = sum_w_value + product("bsd,bse->de", full_in, grad_values)
        sum_b_value = sum_b_value + token_sum(grad_values.astype(jnp.float32))
        input_terms = (
            product("bse,de->bsd", grad_query, w_query)
            + product("bse,de->bsd", grad_keys, w_key)
            + product("bse,de->bsd", grad_values, w_value)
        )
        grad_norm_in = lax.psum_scatter(
            input_terms.astype(jnp.bfloat16), "mp", scatter_dimension=1, tiled=True
        ).astype(jnp.float32)
        sum_ln1_gain = sum_ln1_gain + token_sum(grad_norm_in * unit_in)
        sum_ln1_shift = sum_ln1_shift + token_sum(grad_norm_in)
        input_grads.append(grad_residual + norm_back(grad_norm_in, unit_in, inv_in, ln1_gain))
    totals = tuple(
        lax.psum(
            (
                sum_w_query,
                sum_b_query,
                sum_w_key,
                sum_w_value,
                sum_b_value,
                sum_w_out,
                sum_w_up,
                sum_b_up,
                sum_w_down,
            ),
            "dp",
        )
    )
    common = lax.psum(
        (sum_ln1_gain, sum_ln1_shift, sum_ln2_gain, sum_ln2_shift, sum_b_out, sum_b_down),
        ("dp", "mp"),
    )
    block_out = jnp.concatenate(outputs, axis=0)
    input_grad = jnp.concatenate(input_grads, axis=0)
    return (
        block_out,
        input_grad,
        common[0],
        common[1],
        totals[0],
        totals[1],
        totals[2],
        totals[3],
        totals[4],
        totals[5],
        common[4],
        common[2],
        common[3],
        totals[6],
        totals[7],
        totals[8],
        common[5],
    )


def solution(mesh):
    in_specs = (
        P("dp", "mp", None),
        P("dp"),
        P("dp", "mp", None),
        P(),
        P(),
        P(None, "mp"),
        P("mp"),
        P(None, "mp"),
        P(None, "mp"),
        P("mp"),
        P("mp", None),
        P(),
        P(),
        P(),
        P(None, "mp"),
        P("mp"),
        P("mp", None),
        P(),
    )
    out_specs = (
        P("dp", "mp", None),
        P("dp", "mp", None),
        P(),
        P(),
        P(None, "mp"),
        P("mp"),
        P(None, "mp"),
        P(None, "mp"),
        P("mp"),
        P("mp", None),
        P(),
        P(),
        P(),
        P(None, "mp"),
        P("mp"),
        P("mp", None),
        P(),
    )
    return jax.shard_map(
        on_device, mesh=mesh, in_specs=in_specs, out_specs=out_specs, check_vma=False
    )
```

profile of v0, /device:TPU:0, one launch (start us, length us, event | category | flops | bytes accessed | tf_op | source)
XLA Modules:
  0.0 932.4 jit_solution(8912068039627414131)
XLA Ops:
  12.2 12.8 %all_gather.52 = bf16[1,512,768]{2,1,0:T(8,128)(2,1)S(1)} all-gather(bf16[1,256,768]{2,1,0:T(8,128)(2,1)S(1)} %fusion.127), channel_id=1, replica_groups=mesh['dp'=16,'mp'=2] {'mp'}, dimensions={1}, use_global_device_ids=true | all-gather | bytes 1179648 | tf_op jit(solution)/shard_map/all_gather | solution.py:96
  40.5 16.8 %all_gather.60 = bf16[1,512,768]{2,1,0:T(8,128)(2,1)} all-gather(bf16[1,256,768]{2,1,0:T(8,128)(2,1)S(1)} %get-tuple-element.113), channel_id=1, replica_groups=mesh['dp'=16,'mp'=2] {'mp'}, dimensions={1}, use_global_device_ids=true | all-gather | bytes 1179648 | tf_op jit(solution)/shard_map/all_gather | solution.py:138
  57.3 12.3 %reduce-scatter.25.cloned.1.call-done = f32[1,256,768]{2,1,0:T(8,128)} async-done(((f32[1,512,768]{2,1,0:T(8,128)}), f32[1,256,768]{2,1,0:T(8,128)}) %reduce-scatter.25.cloned.1.call-update) | async-done | bytes 786448 | tf_op jit(solution)/shard_map/reduce_scatter | solution.py:123
  72.2 12.0 %all_gather.53 = bf16[1,512,768]{2,1,0:T(8,128)(2,1)S(1)} all-gather(bf16[1,256,768]{2,1,0:T(8,128)(2,1)S(1)} %add_convert_fusion.7), channel_id=1, replica_groups=mesh['dp'=16,'mp'=2] {'mp'}, dimensions={1}, use_global_device_ids=true | all-gather | bytes 1179648 | tf_op jit(solution)/shard_map/all_gather | solution.py:128
  84.2 10.3 %fusion.16 = (bf16[512,1536]{1,0:T(8,128)(2,1)}, f32[512,1536]{1,0:T(8,128)S(1)}) fusion(f32[1536]{0:T(1024)} %param.33, bf16[768,1536]{1,0:T(8,128)(2,1)S(1)} %copy-done, bf16[1,512,768]{2,1,0:T(8,128)(2,1)S(1)} %all_gather.53), kind=kOutput, calls=%fused_computation.54 | convolution fusion | flops 1259864064 | bytes 7870464 | tf_op jit(solution)/shard_map/bsd,df->bsf/dot_general | solution.py:38
  101.2 4.4 fusion.70
  105.7 22.8 %reduce-scatter.41.cloned.1.call-done = f32[1,256,768]{2,1,0:T(8,128)} async-done(((f32[1,512,768]{2,1,0:T(8,128)}), f32[1,256,768]{2,1,0:T(8,128)}) %reduce-scatter.41.cloned.1.call-update) | async-done | bytes 786448 | tf_op jit(solution)/shard_map/reduce_scatter | solution.py:147
  131.2 17.6 %reduce-scatter.27.cloned.1.call-done = bf16[1,256,768]{2,1,0:T(8,128)(2,1)} async-done(((bf16[1,512,768]{2,1,0:T(8,128)(2,1)}), bf16[1,256,768]{2,1,0:T(8,128)(2,1)}) %reduce-scatter.27.cloned.1.call-update) | async-done | bytes 393232 | tf_op jit(solution)/shard_map/reduce_scatter | solution.py:131
  148.8 3.6 convert_reduce_fusion.14
  152.5 12.1 %all_gather.61 = bf16[1,512,768]{2,1,0:T(8,128)(2,1)S(1)} all-gather(bf16[1,256,768]{2,1,0:T(8,128)(2,1)S(1)} %convert_element_type.620), channel_id=1, replica_groups=mesh['dp'=16,'mp'=2] {'mp'}, dimensions={1}, use_global_device_ids=true | all-gather | bytes 1179648 | tf_op jit(solution)/shard_map/all_gather | solution.py:154
  165.5 4.5 multiply_reduce_fusion.1
  181.2 15.7 %reduce-scatter.43.cloned.1.call-done = bf16[1,256,768]{2,1,0:T(8,128)(2,1)} async-done(((bf16[1,512,768]{2,1,0:T(8,128)(2,1)}), bf16[1,256,768]{2,1,0:T(8,128)(2,1)}) %reduce-scatter.43.cloned.1.call-update) | async-done | bytes 393232 | tf_op jit(solution)/shard_map/reduce_scatter | solution.py:190
  196.9 3.0 fusion.154
  202.5 11.8 %all_gather.54 = bf16[1,512,768]{2,1,0:T(8,128)(2,1)S(1)} all-gather(bf16[1,256,768]{2,1,0:T(8,128)(2,1)S(1)} %get-tuple-element.97), channel_id=1, replica_groups=mesh['dp'=16,'mp'=2] {'mp'}, dimensions={1}, use_global_device_ids=true | all-gather | bytes 1179648 | tf_op jit(solution)/shard_map/all_gather | solution.py:96
  228.0 16.7 %all_gather.50 = bf16[1,512,768]{2,1,0:T(8,128)(2,1)S(1)} all-gather(bf16[1,256,768]{2,1,0:T(8,128)(2,1)} %get-tuple-element.96), channel_id=1, replica_groups=mesh['dp'=16,'mp'=2] {'mp'}, dimensions={1}, use_global_device_ids=true | all-gather | bytes 1179648 | tf_op jit(solution)/shard_map/all_gather | solution.py:96
  259.6 9.8 %all_gather.48 = bf16[1,512,768]{2,1,0:T(8,128)(2,1)S(1)} all-gather(bf16[1,256,768]{2,1,0:T(8,128)(2,1)} %get-tuple-element.95), channel_id=1, replica_groups=mesh['dp'=16,'mp'=2] {'mp'}, dimensions={1}, use_global_device_ids=true | all-gather | bytes 1179648 | tf_op jit(solution)/shard_map/all_gather | solution.py:96
  283.6 10.3 %all_gather.62 = bf16[1,512,768]{2,1,0:T(8,128)(2,1)} all-gather(bf16[1,256,768]{2,1,0:T(8,128)(2,1)} %get-tuple-element.112), channel_id=1, replica_groups=mesh['dp'=16,'mp'=2] {'mp'}, dimensions={1}, use_global_device_ids=true | all-gather | bytes 1179648 | tf_op jit(solution)/shard_map/all_gather | solution.py:138
  293.9 17.9 %all_gather.58 = bf16[1,512,768]{2,1,0:T(8,128)(2,1)} all-gather(bf16[1,256,768]{2,1,0:T(8,128)(2,1)} %get-tuple-element.111), channel_id=1, replica_groups=mesh['dp'=16,'mp'=2] {'mp'}, dimensions={1}, use_global_device_ids=true | all-gather | bytes 1179648 | tf_op jit(solution)/shard_map/all_gather | solution.py:138
  311.8 16.6 %all_gather.56 = bf16[1,512,768]{2,1,0:T(8,128)(2,1)} all-gather(bf16[1,256,768]{2,1,0:T(8,128)(2,1)S(1)} %copy-done.115), channel_id=1, replica_groups=mesh['dp'=16,'mp'=2] {'mp'}, dimensions={1}, use_global_device_ids=true | all-gather | bytes 1179648 | tf_op jit(solution)/shard_map/all_gather | solution.py:138
  332.8 11.8 %all_gather.55 = bf16[1,512,768]{2,1,0:T(8,128)(2,1)} all-gather(bf16[1,256,768]{2,1,0:T(8,128)(2,1)S(1)} %get-tuple-element.120), channel_id=1, replica_groups=mesh['dp'=16,'mp'=2] {'mp'}, dimensions={1}, use_global_device_ids=true | all-gather | bytes 1179648 | tf_op jit(solution)/shard_map/all_gather | solution.py:128
  344.7 10.9 %all_gather.51 = bf16[1,512,768]{2,1,0:T(8,128)(2,1)S(1)} all-gather(bf16[1,256,768]{2,1,0:T(8,128)(2,1)S(1)} %get-tuple-element.119), channel_id=1, replica_groups=mesh['dp'=16,'mp'=2] {'mp'}, dimensions={1}, use_global_device_ids=true | all-gather | bytes 1179648 | tf_op jit(solution)/shard_map/all_gather | solution.py:128
  355.6 9.4 %fusion.13 = (bf16[512,1536]{1,0:T(8,128)(2,1)}, f32[512,1536]{1,0:T(8,128)S(1)}) fusion(f32[1536]{0:T(1024)S(1)} %copy-done.189, bf16[768,1536]{1,0:T(8,128)(2,1)S(1)} %copy-done, bf16[1,512,768]{2,1,0:T(8,128)(2,1)S(1)} %all_gather.51), kind=kOutput, calls=%fused_computation.51 | convolution fusion | flops 1259864064 | bytes 7870464 | tf_op jit(solution)/shard_map/bsd,df->bsf/dot_general | solution.py:38
  365.0 10.5 %all_gather.49 = bf16[1,512,768]{2,1,0:T(8,128)(2,1)} all-gather(bf16[1,256,768]{2,1,0:T(8,128)(2,1)S(1)} %get-tuple-element.118), channel_id=1, replica_groups=mesh['dp'=16,'mp'=2] {'mp'}, dimensions={1}, use_global_device_ids=true | all-gather | bytes 1179648 | tf_op jit(solution)/shard_map/all_gather | solution.py:128
  382.2 9.8 %fusion.19 = (bf16[512,1536]{1,0:T(8,128)(2,1)}, f32[512,1536]{1,0:T(8,128)S(1)}) fusion(f32[1536]{0:T(1024)S(1)} %copy-done.189, bf16[768,1536]{1,0:T(8,128)(2,1)S(1)} %copy-done, bf16[1,512,768]{2,1,0:T(8,128)(2,1)} %all_gather.55), kind=kOutput, calls=%fused_computation.57 | convolution fusion | flops 1259864064 | bytes 7870464 | tf_op jit(solution)/shard_map/bsd,df->bsf/dot_general | solution.py:38
  398.9 9.8 %fusion.10 = (bf16[512,1536]{1,0:T(8,128)(2,1)}, f32[512,1536]{1,0:T(8,128)S(1)}) fusion(f32[1536]{0:T(1024)S(1)} %copy-done.189, bf16[768,1536]{1,0:T(8,128)(2,1)S(1)} %copy-done, bf16[1,512,768]{2,1,0:T(8,128)(2,1)} %all_gather.49), kind=kOutput, calls=%fused_computation.48 | convolution fusion | flops 1259864064 | bytes 7870464 | tf_op jit(solution)/shard_map/bsd,df->bsf/dot_general | solution.py:38
  415.4 4.5 fusion.68
  420.0 5.4 fusion.162
  425.4 3.6 fusion.184
  429.1 3.5 fusion.173
  435.2 5.4 fusion.193
  440.6 3.6 fusion.202
  444.2 3.6 fusion.167
  450.2 9.8 %add_add_fusion = f32[1536,768]{1,0:T(8,128)} fusion(f32[1536,768]{1,0:T(8,128)} %fusion.162, f32[1536,768]{1,0:T(8,128)} %fusion.173, f32[1536,768]{1,0:T(8,128)} %fusion.167, bf16[512,1536]{1,0:T(8,128)(2,1)} %get-tuple-element.145, bf16[1,512,768]{2,1,0:T(8,128)(2,1)} %all_gather.62), kind=kOutput, calls=%fused_computation.32 | convolution fusion | flops 1211498496 | bytes 21233664 | tf_op jit(solution)/shard_map/bsf,bsd->fd/dot_general | solution.py:38
  460.0 9.1 add_add_fusion.1
  469.1 3.7 multiply_reduce_fusion.7
  472.8 13.2 %reduce-scatter.19.cloned.1.call-done = bf16[1,256,768]{2,1,0:T(8,128)(2,1)} async-done(((bf16[1,512,768]{2,1,0:T(8,128)(2,1)}), bf16[1,256,768]{2,1,0:T(8,128)(2,1)}) %reduce-scatter.19.cloned.1.call-update) | async-done | bytes 393232 | tf_op jit(solution)/shard_map/reduce_scatter | solution.py:131
  486.1 20.2 %reduce-scatter.31.cloned.1.call-done = bf16[1,256,768]{2,1,0:T(8,128)(2,1)} async-done(((bf16[1,512,768]{2,1,0:T(8,128)(2,1)}), bf16[1,256,768]{2,1,0:T(8,128)(2,1)}) %reduce-scatter.31.cloned.1.call-update) | async-done | bytes 393232 | tf_op jit(solution)/shard_map/reduce_scatter | solution.py:131
  506.3 4.9 fusion.215
  511.3 19.5 %all_gather.57 = bf16[1,512,768]{2,1,0:T(8,128)(2,1)S(1)} all-gather(bf16[1,256,768]{2,1,0:T(8,128)(2,1)S(1)} %convert_element_type.586), channel_id=1, replica_groups=mesh['dp'=16,'mp'=2] {'mp'}, dimensions={1}, use_global_device_ids=true | all-gather | bytes 1179648 | tf_op jit(solution)/shard_map/all_gather | solution.py:154
  544.6 3.2 fusion.214
  547.8 8.5 all_gather.59
  557.2 4.6 multiply_reduce_fusion.2
  568.1 8.6 all_gather.63
  609.5 3.7 fusion.75
  642.5 60.4 %all-reduce.1 = (f32[384]{0:T(512)}, f32[384]{0:T(512)}, f32[1536]{0:T(1024)}) all-reduce(f32[384]{0:T(512)} %add.700, f32[384]{0:T(512)} %add.710, f32[1536]{0:T(1024)S(1)} %add_add_fusion.2), channel_id=1, replica_groups=mesh['dp'=16,'mp'=2] {'dp'}, use_global_device_ids=true, to_apply=%region_75.76 | all-reduce | flops 2304 | bytes 18432 | tf_op jit(solution)/shard_map/psum | solution.py:197
  707.3 3.6 fusion.155
  713.4 39.4 %all-reduce = (f32[768]{0:T(1024)}, f32[768]{0:T(1024)}, f32[768]{0:T(1024)}, f32[768]{0:T(1024)}, f32[768]{0:T(1024)}, /*index=5*/f32[768]{0:T(1024)}) all-reduce(f32[768]{0:T(1024)} %add_add_fusion.10, f32[768]{0:T(1024)} %add_add_fusion.9, f32[768]{0:T(1024)} %add_add_fusion.6, ...), channel_id=1, replica_groups=mesh['dp'=16,'mp'=2] {'dp','mp'}, use_global_device_ids=true, to_apply=%region_64.65 | all-reduce | flops 4608 | bytes 36864 | tf_op jit(solution)/shard_map/psum | solution.py:212
  763.1 151.8 %all-reduce.5.cloned.1.call-done = (f32[768,384]{1,0:T(8,128)}, f32[768,384]{1,0:T(8,128)}, f32[768,384]{1,0:T(8,128)}, f32[384,768]{1,0:T(8,128)}, f32[768,1536]{1,0:T(8,128)}, /*index=5*/f32[1536,768]{1,0:T(8,128)}) async-done(((f32[768,384]{1,0:T(8,128)}, f32[768,384]{1,0:T(8,128)}, f32[768,384]{1,0:T(8,128)}, f32[384,768]{1,0:T(8,128)}, f32[768,1536]{1,0:T(8,128)}, /*index=5*/f32[1536,768]{1,0:T(8,128)}), ...) | async-done | bytes 14155792 | tf_op jit(solution)/shard_map/psum | solution.py:197
  (630 shorter events, 228.7 us)
Async XLA Ops:
  7.2 77.0 %copy-start = (bf16[768,1536]{1,0:T(8,128)(2,1)S(1)}, bf16[768,1536]{1,0:T(8,128)(2,1)}, u32[]{:S(2)}) copy-start(bf16[768,1536]{1,0:T(8,128)(2,1)} %param.32) | copy-start | bytes 7077892
  7.2 19.1 %copy-start.35 = (bf16[768,384]{1,0:T(8,128)(2,1)S(1)}, bf16[768,384]{1,0:T(8,128)(2,1)}, u32[]{:S(2)}) copy-start(bf16[768,384]{1,0:T(8,128)(2,1)} %param.25) | copy-start | bytes 1769476
  7.2 19.7 %copy-start.38 = (bf16[768,384]{1,0:T(8,128)(2,1)S(1)}, bf16[768,384]{1,0:T(8,128)(2,1)}, u32[]{:S(2)}) copy-start(bf16[768,384]{1,0:T(8,128)(2,1)} %param.23) | copy-start | bytes 1769476
  7.2 19.7 %copy-start.190 = (f32[384]{0:T(512)S(1)}, f32[384]{0:T(512)}, u32[]{:S(2)}) copy-start(f32[384]{0:T(512)} %param.24) | copy-start | bytes 4612
  7.2 62.3 %reduce-scatter.25.cloned.1.call-start = ((), (), s32[]{:S(2)}) async-start(), calls=%async_computation.20 | async-start | bytes 2359296 | tf_op jit(solution)/shard_map/reduce_scatter | solution.py:123
  38.0 90.5 %reduce-scatter.41.cloned.1.call-start = ((), (), s32[]{:S(2)}) async-start(), calls=%async_computation.28 | async-start | bytes 2359296 | tf_op jit(solution)/shard_map/reduce_scatter | solution.py:147
  101.1 47.7 %reduce-scatter.27.cloned.1.call-start = ((), (), s32[]{:S(2)}) async-start(), calls=%async_computation.21 | async-start | bytes 1179648 | tf_op jit(solution)/shard_map/reduce_scatter | solution.py:131
  105.6 91.3 %reduce-scatter.43.cloned.1.call-start = ((), (), s32[]{:S(2)}) async-start(), calls=%async_computation.29 | async-start | bytes 1179648 | tf_op jit(solution)/shard_map/reduce_scatter | solution.py:190
  177.8 19.2 %copy-start.140 = (f32[768]{0:T(1024)S(1)}, f32[768]{0:T(1024)}, u32[]{:S(2)}) copy-start(f32[768]{0:T(1024)} %param.21) | copy-start | bytes 9220
  179.3 149.1 %reduce-scatter.29.cloned.1.call-start = ((), (), s32[]{:S(2)}) async-start(), calls=%async_computation.22 | async-start | bytes 2359296 | tf_op jit(solution)/shard_map/reduce_scatter | solution.py:123
  180.5 35.0 %copy-start.144 = (f32[256]{0:T(256)}, f32[256]{0:T(256)S(1)}, u32[]{:S(2)}) copy-start(f32[256]{0:T(256)S(1)} %broadcast_multiply_fusion.17) | copy-start | bytes 3076
  181.2 34.4 %copy-start.147 = (f32[256]{0:T(256)}, f32[256]{0:T(256)S(1)}, u32[]{:S(2)}) copy-start(f32[256]{0:T(256)S(1)} %get-tuple-element.181) | copy-start | bytes 3076
  181.2 34.4 %copy-start.148 = (f32[256]{0:T(256)}, f32[256]{0:T(256)S(1)}, u32[]{:S(2)}) copy-start(f32[256]{0:T(256)S(1)} %get-tuple-element.182) | copy-start | bytes 3076
  225.5 21.2 %copy-start.191 = (f32[384]{0:T(512)S(1)}, f32[384]{0:T(512)}, u32[]{:S(2)}) copy-start(f32[384]{0:T(512)} %param.24) | copy-start | bytes 4612
  227.3 101.2 %reduce-scatter.21.cloned.1.call-start = ((), (), s32[]{:S(2)}) async-start(), calls=%async_computation.18 | async-start | bytes 2359296 | tf_op jit(solution)/shard_map/reduce_scatter | solution.py:123
  228.0 24.0 %copy-start.175 = (pred[512]{0:T(512)(128)(4,1)}, pred[512]{0:T(512)(128)(4,1)S(1)}, u32[]{:S(2)}) copy-start(pred[512]{0:T(512)(128)(4,1)S(1)} %iota_compare_fusion.2) | copy-start | bytes 1540
  258.8 70.4 %reduce-scatter.17.cloned.1.call-start = ((), (), s32[]{:S(2)}) async-start(), calls=%async_computation.16 | async-start | bytes 2359296 | tf_op jit(solution)/shard_map/reduce_scatter | solution.py:123
  281.7 30.1 %copy-start.115 = (bf16[1,256,768]{2,1,0:T(8,128)(2,1)S(1)}, bf16[1,256,768]{2,1,0:T(8,128)(2,1)}, u32[]{:S(2)}) copy-start(bf16[1,256,768]{2,1,0:T(8,128)(2,1)} %get-tuple-element.110) | copy-start | bytes 1179652
  283.5 45.7 %copy-start.166 = (f32[768]{0:T(1024)S(1)}, f32[768]{0:T(1024)}, u32[]{:S(2)}) copy-start(f32[768]{0:T(1024)} %param.29) | copy-start | bytes 9220
  283.5 185.6 %reduce-scatter.37.cloned.1.call-start = ((), (), s32[]{:S(2)}) async-start(), calls=%async_computation.26 | async-start | bytes 2359296 | tf_op jit(solution)/shard_map/reduce_scatter | solution.py:147
  331.8 137.2 %copy-start.146 = (f32[256]{0:T(256)}, f32[256]{0:T(256)S(1)}, u32[]{:S(2)}) copy-start(f32[256]{0:T(256)S(1)} %broadcast_multiply_fusion.20) | copy-start | bytes 3076
  332.1 137.0 %copy-start.172 = (f32[256]{0:T(256)}, f32[256]{0:T(256)S(1)}, u32[]{:S(2)}) copy-start(f32[256]{0:T(256)S(1)} %add_rsqrt_fusion.4) | copy-start | bytes 3076
  332.3 23.2 %copy-start.189 = (f32[1536]{0:T(1024)S(1)}, f32[1536]{0:T(1024)}, u32[]{:S(2)}) copy-start(f32[1536]{0:T(1024)} %param.33) | copy-start | bytes 18436
  355.6 20.0 %copy-start.85 = (bf16[1,512,768]{2,1,0:T(8,128)(2,1)S(1)}, bf16[1,512,768]{2,1,0:T(8,128)(2,1)}, u32[]{:S(2)}) copy-start(bf16[1,512,768]{2,1,0:T(8,128)(2,1)} %all_gather.58) | copy-start | bytes 2359300
  355.6 20.0 %copy-start.184 = (bf16[1536,768]{1,0:T(8,128)(2,1)S(1)}, bf16[1536,768]{1,0:T(8,128)(2,1)}, u32[]{:S(2)}) copy-start(bf16[1536,768]{1,0:T(8,128)(2,1)} %param.34) | copy-start | bytes 7077892
  382.1 87.0 %reduce-scatter.45.cloned.1.call-start = ((), (), s32[]{:S(2)}) async-start(), calls=%async_computation.30 | async-start | bytes 2359296 | tf_op jit(solution)/shard_map/reduce_scatter | solution.py:147
  398.6 70.4 %reduce-scatter.33.cloned.1.call-start = ((), (), s32[]{:S(2)}) async-start(), calls=%async_computation.24 | async-start | bytes 2359296 | tf_op jit(solution)/shard_map/reduce_scatter | solution.py:147
  415.3 70.8 %reduce-scatter.19.cloned.1.call-start = ((), (), s32[]{:S(2)}) async-start(), calls=%async_computation.17 | async-start | bytes 1179648 | tf_op jit(solution)/shard_map/reduce_scatter | solution.py:131
  419.9 86.4 %reduce-scatter.31.cloned.1.call-start = ((), (), s32[]{:S(2)}) async-start(), calls=%async_computation.23 | async-start | bytes 1179648 | tf_op jit(solution)/shard_map/reduce_scatter | solution.py:131
  434.9 109.7 %reduce-scatter.23.cloned.1.call-start = ((), (), s32[]{:S(2)}) async-start(), calls=%async_computation.19 | async-start | bytes 1179648 | tf_op jit(solution)/shard_map/reduce_scatter | solution.py:131
  450.2 257.0 %reduce-scatter.35.cloned.1.call-start = ((), (), s32[]{:S(2)}) async-start(), calls=%async_computation.25 | async-start | bytes 1179648 | tf_op jit(solution)/shard_map/reduce_scatter | solution.py:190
  469.1 37.2 %copy-start.142 = (f32[768]{0:T(1024)S(1)}, f32[768]{0:T(1024)}, u32[]{:S(2)}) copy-start(f32[768]{0:T(1024)} %param.35) | copy-start | bytes 9220
  506.3 24.5 %copy-start.33 = (bf16[384,768]{1,0:T(8,128)(2,1)S(1)}, bf16[384,768]{1,0:T(8,128)(2,1)}, u32[]{:S(2)}) copy-start(bf16[384,768]{1,0:T(8,128)(2,1)} %param.28) | copy-start | bytes 1769476
  506.3 27.4 %slice-start.4 = ((s8[6291456]{0:T(1024)(128)(4,1)}), s8[4194304]{0:T(1024)(128)(4,1)S(1)}, s32[]{:S(2)}) async-start(s8[6291456]{0:T(1024)(128)(4,1)} %bitcast.416), calls=%async_computation.37 | async-start | bytes 8388608
  511.2 22.5 %copy-start.48 = (f32[1,256,768]{2,1,0:T(8,128)}, f32[1,256,768]{2,1,0:T(8,128)S(1)}, u32[]{:S(2)}) copy-start(f32[1,256,768]{2,1,0:T(8,128)S(1)} %get-tuple-element.82) | copy-start | bytes 2359300
  511.2 20.0 %copy-start.11 = (bf16[6,512,512]{1,2,0:T(8,128)(2,1)S(1)}, bf16[6,512,512]{1,2,0:T(8,128)(2,1)}, u32[]{:S(2)}) copy-start(bf16[6,512,512]{1,2,0:T(8,128)(2,1)} %copy-done.10) | copy-start | bytes 9437188
  511.2 22.5 %slice-start.5 = ((s8[6291456]{0:T(1024)(128)(4,1)}), s8[2097152]{0:T(1024)(128)(4,1)S(1)}, s32[]{:S(2)}) async-start(s8[6291456]{0:T(1024)(128)(4,1)} %bitcast.416), calls=%async_computation.38 | async-start | bytes 4194304
  588.7 118.5 %reduce-scatter.39.cloned.1.call-start = ((), (), s32[]{:S(2)}) async-start(), calls=%async_computation.27 | async-start | bytes 1179648 | tf_op jit(solution)/shard_map/reduce_scatter | solution.py:190
  609.2 98.0 %reduce-scatter.47.cloned.1.call-start = ((), (), s32[]{:S(2)}) async-start(), calls=%async_computation.31 | async-start | bytes 1179648 | tf_op jit(solution)/shard_map/reduce_scatter | solution.py:190
  623.6 291.2 %all-reduce.5.cloned.1.call-start = ((), (), s32[]{:S(2)}) async-start(), calls=%async_computation.32 | async-start | bytes 28311552 | tf_op jit(solution)/shard_map/psum | solution.py:197
  632.0 71.0 %copy-start.105 = (bf16[1,256,768]{2,1,0:T(8,128)(2,1)S(1)}, bf16[1,256,768]{2,1,0:T(8,128)(2,1)}, u32[]{:S(2)}) copy-start(bf16[1,256,768]{2,1,0:T(8,128)(2,1)} %get-tuple-element.114) | copy-start | bytes 1179652
  632.0 71.0 %copy-start.112 = (bf16[1,256,768]{2,1,0:T(8,128)(2,1)S(1)}, bf16[1,256,768]{2,1,0:T(8,128)(2,1)}, u32[]{:S(2)}) copy-start(bf16[1,256,768]{2,1,0:T(8,128)(2,1)} %get-tuple-element.117) | copy-start | bytes 1179652
  632.0 71.0 %copy-start.116 = (bf16[1,256,768]{2,1,0:T(8,128)(2,1)S(1)}, bf16[1,256,768]{2,1,0:T(8,128)(2,1)}, u32[]{:S(2)}) copy-start(bf16[1,256,768]{2,1,0:T(8,128)(2,1)} %get-tuple-element.115) | copy-start | bytes 1179652
  632.0 75.2 %copy-start.141 = (f32[768]{0:T(1024)S(1)}, f32[768]{0:T(1024)}, u32[]{:S(2)}) copy-start(f32[768]{0:T(1024)} %param.21) | copy-start | bytes 9220
  632.0 75.2 %copy-start.145 = (f32[256]{0:T(256)S(1)}, f32[256]{0:T(256)}, u32[]{:S(2)}) copy-start(f32[256]{0:T(256)} %copy-done.144) | copy-start | bytes 3076
  707.2 52.6 %copy-start.44 = (f32[1,256,768]{2,1,0:T(8,128)S(1)}, f32[1,256,768]{2,1,0:T(8,128)}, u32[]{:S(2)}) copy-start(f32[1,256,768]{2,1,0:T(8,128)} %copy-done.43) | copy-start | bytes 2359300
  707.2 52.7 %copy-start.150 = (f32[256]{0:T(256)S(1)}, f32[256]{0:T(256)}, u32[]{:S(2)}) copy-start(f32[256]{0:T(256)} %copy-done.149) | copy-start | bytes 3076
  707.2 52.6 %copy-start.117 = (bf16[1,256,768]{2,1,0:T(8,128)(2,1)S(1)}, bf16[1,256,768]{2,1,0:T(8,128)(2,1)}, u32[]{:S(2)}) copy-start(bf16[1,256,768]{2,1,0:T(8,128)(2,1)} %reduce-scatter.47.cloned.1.call-done) | copy-start | bytes 1179652
  (175 other events, 866.9 us)
Sparse Core Ops, SparseCore 0:
  38.1 31.3 reduce-scatter.24
  101.3 27.2 reduce-scatter.40
  131.3 17.4 reduce-scatter.26
  179.4 17.4 reduce-scatter.42
  227.4 29.7 reduce-scatter.28
  260.0 29.1 reduce-scatter.20
  292.0 37.1 reduce-scatter.16
  382.2 26.8 reduce-scatter.36
  411.4 26.0 reduce-scatter.44
  439.7 26.0 reduce-scatter.32
  468.6 17.4 reduce-scatter.18
  488.8 17.4 reduce-scatter.30
  509.1 23.6 reduce-scatter.22
  588.8 17.3 reduce-scatter.34
  609.3 17.3 reduce-scatter.38
  629.5 17.4 reduce-scatter.46
  653.1 261.7 all-reduce.4
where the time goes:
time: 940 us; the launch traced here: 932 us
  blocking collectives  307 us (33%)
  waiting for transfers between devices  255 us (27%)
  matrix products  229 us (24%)
  other arithmetic  87.3 us (9%)
  local copies, waits for them, and re-layouts  37.1 us (4%)
  between operations  16.6 us (2%)
    dot_general x96, matrix products, product(): jnp.einsum(pattern, left_side, right_side, preferred_element_type=jnp.flo...  229 us
    psum x1, waiting for transfers between devices, on_device(): lax.psum((sum_w_query, sum_b_query, sum_w_key, sum_w_value, sum_b_value,...  152 us
    all_gather x4, blocking collectives, on_device(): grad_full = lax.all_gather(upstream, 'mp', axis=1, tiled=True)  61.7 us
    psum x1, blocking collectives, on_device(): lax.psum((sum_w_query, sum_b_query, sum_w_key, sum_w_value, sum_b_value,...  60.4 us
    all_gather x4, blocking collectives, on_device(): lax.all_gather(normed_in.astype(jnp.bfloat16), 'mp', axis=1, tiled=True)  51.1 us
    reduce_scatter x4, waiting for transfers between devices, on_device(): lax.psum_scatter(product('bsf,fd->bsd', active, w_down).astype(jnp.bfloat...  51 us
    all_gather x4, blocking collectives, on_device(): lax.all_gather(grad_residual.astype(jnp.bfloat16), 'mp', axis=1, tiled=True)  48.7 us
    all_gather x4, blocking collectives, on_device(): lax.all_gather(normed_mid.astype(jnp.bfloat16), 'mp', axis=1, tiled=True)  45.3 us
  transfers between devices with their start and end apart: 17, of which 8 were waited for; matrix products, arithmetic and copies ran while one was open for 23% of the time, Pallas kernels for 0%

commit v1 on v0

--- a/solution.py
+++ b/solution.py
@@ -10,6 +10,11 @@
 ROWS_MB = 1
 epsilon = 1e-12
 masked_fill = -1000000000.0
+
+
+def by_each_axis(value, one, other):
+    half = lax.psum(value, one)
+    return lax.psum(half, other)
 
 
 def layer_norm(values, gain_vec, offset):
@@ -209,9 +214,10 @@
             "dp",
         )
     )
-    common = lax.psum(
+    common = by_each_axis(
         (sum_ln1_gain, sum_ln1_shift, sum_ln2_gain, sum_ln2_shift, sum_b_out, sum_b_down),
-        ("dp", "mp"),
+        "mp",
+        "dp",
     )
     block_out = jnp.concatenate(outputs, axis=0)
     input_grad = jnp.concatenate(input_grads, axis=0)

time: 940 us -> 942 us (level)
  waiting for transfers between devices: 255 us -> 272 us
  blocking collectives: 307 us -> 293 us
    psum x2, blocking collectives: 99.8 us -> 72.8 us  [the longest x1 64.5 us: by_each_axis(): return lax.psum(half, other)]
    psum x1, waiting for transfers between devices: 152 us -> 178 us  [on_device(): lax.psum((sum_w_query, sum_b_query, sum_w_key, sum_w_value, sum_b_value,...]
    all_gather x4, blocking collectives: 45.3 us -> 58.9 us  [on_device(): lax.all_gather(normed_mid.astype(jnp.bfloat16), 'mp', axis=1, tiled=True)]
    reduce_scatter x4, waiting for transfers between devices: 51 us -> 39.6 us  [on_device(): lax.psum_scatter(product('bsf,fd->bsd', active, w_down).astype(jnp.bfloat...]
    unnamed x418 -> x448, local copies, waits for them, and re-layouts: 31.2 us -> 31.5 us
  transfers between devices with their start and end apart: 17 -> 17, of which waited for: 8 -> 9; matrix products, arithmetic and copies ran while one was open for 23% -> 22% of each run, Pallas kernels for 0% -> 0%
where the time goes in v1:
time: 942 us; the launch traced here: 934 us
  blocking collectives  293 us (31%)
  waiting for transfers between devices  272 us (29%)
  matrix products  224 us (24%)
  other arithmetic  88.4 us (9%)
  local copies, waits for them, and re-layouts  37.3 us (4%)
  between operations  16.7 us (2%)
    dot_general x96, matrix products, product(): jnp.einsum(pattern, left_side, right_side, preferred_element_type=jnp.flo...  224 us
    psum x1, waiting for transfers between devices, on_device(): lax.psum((sum_w_query, sum_b_query, sum_w_key, sum_w_value, sum_b_value,...  178 us
    psum x1, blocking collectives, by_each_axis(): return lax.psum(half, other)  64.5 us
    all_gather x4, blocking collectives, on_device(): grad_full = lax.all_gather(upstream, 'mp', axis=1, tiled=True)  62.4 us
    all_gather x4, blocking collectives, on_device(): lax.all_gather(normed_mid.astype(jnp.bfloat16), 'mp', axis=1, tiled=True)  58.9 us
    all_gather x4, blocking collectives, on_device(): lax.all_gather(normed_in.astype(jnp.bfloat16), 'mp', axis=1, tiled=True)  50.9 us
    all_gather x4, blocking collectives, on_device(): lax.all_gather(grad_residual.astype(jnp.bfloat16), 'mp', axis=1, tiled=True)  48.2 us
    reduce_scatter x4, waiting for transfers between devices, on_device(): lax.psum_scatter(product('bsf,fd->bsd', active, w_down).astype(jnp.bfloat...  39.6 us
  transfers between devices with their start and end apart: 17, of which 9 were waited for; matrix products, arithmetic and copies ran while one was open for 22% of the time, Pallas kernels for 0%

profile of v1, /device:TPU:0, one launch (start us, length us, event | category | flops | bytes accessed | tf_op | source)
XLA Modules:
  0.0 934.0 jit_solution(2510134234578043178)
XLA Ops:
  12.2 12.8 %all_gather.52 = bf16[1,512,768]{2,1,0:T(8,128)(2,1)S(1)} all-gather(bf16[1,256,768]{2,1,0:T(8,128)(2,1)S(1)} %fusion.127), channel_id=1, replica_groups=mesh['dp'=16,'mp'=2] {'mp'}, dimensions={1}, use_global_device_ids=true | all-gather | bytes 1179648 | tf_op jit(solution)/shard_map/all_gather | solution.py:101
  40.4 16.8 %all_gather.60 = bf16[1,512,768]{2,1,0:T(8,128)(2,1)} all-gather(bf16[1,256,768]{2,1,0:T(8,128)(2,1)S(1)} %get-tuple-element.119), channel_id=1, replica_groups=mesh['dp'=16,'mp'=2] {'mp'}, dimensions={1}, use_global_device_ids=true | all-gather | bytes 1179648 | tf_op jit(solution)/shard_map/all_gather | solution.py:143
  57.2 12.3 %reduce-scatter.25.cloned.1.call-done = f32[1,256,768]{2,1,0:T(8,128)} async-done(((f32[1,512,768]{2,1,0:T(8,128)}), f32[1,256,768]{2,1,0:T(8,128)}) %reduce-scatter.25.cloned.1.call-update) | async-done | bytes 786448 | tf_op jit(solution)/shard_map/reduce_scatter | solution.py:128
  72.1 12.1 %all_gather.53 = bf16[1,512,768]{2,1,0:T(8,128)(2,1)S(1)} all-gather(bf16[1,256,768]{2,1,0:T(8,128)(2,1)S(1)} %add_convert_fusion.7), channel_id=1, replica_groups=mesh['dp'=16,'mp'=2] {'mp'}, dimensions={1}, use_global_device_ids=true | all-gather | bytes 1179648 | tf_op jit(solution)/shard_map/all_gather | solution.py:133
  84.1 10.3 %fusion.16 = (bf16[512,1536]{1,0:T(8,128)(2,1)}, f32[512,1536]{1,0:T(8,128)S(1)}) fusion(f32[1536]{0:T(1024)} %param.33, bf16[768,1536]{1,0:T(8,128)(2,1)S(1)} %copy-done, bf16[1,512,768]{2,1,0:T(8,128)(2,1)S(1)} %all_gather.53), kind=kOutput, calls=%fused_computation.54 | convolution fusion | flops 1259864064 | bytes 7870464 | tf_op jit(solution)/shard_map/bsd,df->bsf/dot_general | solution.py:43
  101.0 4.4 fusion.70
  105.5 22.8 %reduce-scatter.41.cloned.1.call-done = f32[1,256,768]{2,1,0:T(8,128)} async-done(((f32[1,512,768]{2,1,0:T(8,128)}), f32[1,256,768]{2,1,0:T(8,128)}) %reduce-scatter.41.cloned.1.call-update) | async-done | bytes 786448 | tf_op jit(solution)/shard_map/reduce_scatter | solution.py:152
  131.1 17.6 %reduce-scatter.27.cloned.1.call-done = bf16[1,256,768]{2,1,0:T(8,128)(2,1)} async-done(((bf16[1,512,768]{2,1,0:T(8,128)(2,1)}), bf16[1,256,768]{2,1,0:T(8,128)(2,1)}) %reduce-scatter.27.cloned.1.call-update) | async-done | bytes 393232 | tf_op jit(solution)/shard_map/reduce_scatter | solution.py:136
  148.7 3.6 convert_reduce_fusion.14
  152.3 12.0 %all_gather.61 = bf16[1,512,768]{2,1,0:T(8,128)(2,1)S(1)} all-gather(bf16[1,256,768]{2,1,0:T(8,128)(2,1)S(1)} %convert_element_type.620), channel_id=1, replica_groups=mesh['dp'=16,'mp'=2] {'mp'}, dimensions={1}, use_global_device_ids=true | all-gather | bytes 1179648 | tf_op jit(solution)/shard_map/all_gather | solution.py:159
  167.0 4.6 multiply_reduce_fusion.1
  181.1 15.5 %reduce-scatter.43.cloned.1.call-done = bf16[1,256,768]{2,1,0:T(8,128)(2,1)} async-done(((bf16[1,512,768]{2,1,0:T(8,128)(2,1)}), bf16[1,256,768]{2,1,0:T(8,128)(2,1)}) %reduce-scatter.43.cloned.1.call-update) | async-done | bytes 393232 | tf_op jit(solution)/shard_map/reduce_scatter | solution.py:195
  196.6 2.9 fusion.154
  202.2 12.2 %all_gather.48 = bf16[1,512,768]{2,1,0:T(8,128)(2,1)S(1)} all-gather(bf16[1,256,768]{2,1,0:T(8,128)(2,1)S(1)} %get-tuple-element.101), channel_id=1, replica_groups=mesh['dp'=16,'mp'=2] {'mp'}, dimensions={1}, use_global_device_ids=true | all-gather | bytes 1179648 | tf_op jit(solution)/shard_map/all_gather | solution.py:101
  227.9 16.6 %all_gather.50 = bf16[1,512,768]{2,1,0:T(8,128)(2,1)S(1)} all-gather(bf16[1,256,768]{2,1,0:T(8,128)(2,1)} %get-tuple-element.102), channel_id=1, replica_groups=mesh['dp'=16,'mp'=2] {'mp'}, dimensions={1}, use_global_device_ids=true | all-gather | bytes 1179648 | tf_op jit(solution)/shard_map/all_gather | solution.py:101
  259.2 9.3 all_gather.54
  282.7 10.8 %all_gather.56 = bf16[1,512,768]{2,1,0:T(8,128)(2,1)} all-gather(bf16[1,256,768]{2,1,0:T(8,128)(2,1)} %get-tuple-element.116), channel_id=1, replica_groups=mesh['dp'=16,'mp'=2] {'mp'}, dimensions={1}, use_global_device_ids=true | all-gather | bytes 1179648 | tf_op jit(solution)/shard_map/all_gather | solution.py:143
  293.5 18.9 %all_gather.62 = bf16[1,512,768]{2,1,0:T(8,128)(2,1)} all-gather(bf16[1,256,768]{2,1,0:T(8,128)(2,1)} %get-tuple-element.118), channel_id=1, replica_groups=mesh['dp'=16,'mp'=2] {'mp'}, dimensions={1}, use_global_device_ids=true | all-gather | bytes 1179648 | tf_op jit(solution)/shard_map/all_gather | solution.py:143
  312.4 15.9 %all_gather.58 = bf16[1,512,768]{2,1,0:T(8,128)(2,1)} all-gather(bf16[1,256,768]{2,1,0:T(8,128)(2,1)S(1)} %copy-done.121), channel_id=1, replica_groups=mesh['dp'=16,'mp'=2] {'mp'}, dimensions={1}, use_global_device_ids=true | all-gather | bytes 1179648 | tf_op jit(solution)/shard_map/all_gather | solution.py:143
  333.8 12.0 %all_gather.49 = bf16[1,512,768]{2,1,0:T(8,128)(2,1)S(1)} all-gather(bf16[1,256,768]{2,1,0:T(8,128)(2,1)S(1)} %get-tuple-element.124), channel_id=1, replica_groups=mesh['dp'=16,'mp'=2] {'mp'}, dimensions={1}, use_global_device_ids=true | all-gather | bytes 1179648 | tf_op jit(solution)/shard_map/all_gather | solution.py:133
  345.8 9.4 %fusion.10 = (bf16[512,1536]{1,0:T(8,128)(2,1)}, f32[512,1536]{1,0:T(8,128)S(1)}) fusion(f32[1536]{0:T(1024)S(1)} %copy-done.203, bf16[768,1536]{1,0:T(8,128)(2,1)S(1)} %copy-done, bf16[1,512,768]{2,1,0:T(8,128)(2,1)S(1)} %all_gather.49), kind=kOutput, calls=%fused_computation.48 | convolution fusion | flops 1259864064 | bytes 7870464 | tf_op jit(solution)/shard_map/bsd,df->bsf/dot_general | solution.py:43
  361.9 15.7 %all_gather.55 = bf16[1,512,768]{2,1,0:T(8,128)(2,1)S(1)} all-gather(bf16[1,256,768]{2,1,0:T(8,128)(2,1)} %get-tuple-element.126), channel_id=1, replica_groups=mesh['dp'=16,'mp'=2] {'mp'}, dimensions={1}, use_global_device_ids=true | all-gather | bytes 1179648 | tf_op jit(solution)/shard_map/all_gather | solution.py:133
  377.6 19.1 %all_gather.51 = bf16[1,512,768]{2,1,0:T(8,128)(2,1)} all-gather(bf16[1,256,768]{2,1,0:T(8,128)(2,1)S(1)} %get-tuple-element.125), channel_id=1, replica_groups=mesh['dp'=16,'mp'=2] {'mp'}, dimensions={1}, use_global_device_ids=true | all-gather | bytes 1179648 | tf_op jit(solution)/shard_map/all_gather | solution.py:133
  396.7 10.3 %fusion.19 = (bf16[512,1536]{1,0:T(8,128)(2,1)}, f32[512,1536]{1,0:T(8,128)S(1)}) fusion(f32[1536]{0:T(1024)} %param.33, bf16[768,1536]{1,0:T(8,128)(2,1)S(1)} %copy-done, bf16[1,512,768]{2,1,0:T(8,128)(2,1)S(1)} %all_gather.55), kind=kOutput, calls=%fused_computation.57 | convolution fusion | flops 1259864064 | bytes 7870464 | tf_op jit(solution)/shard_map/bsd,df->bsf/dot_general | solution.py:43
  414.1 9.8 %fusion.13 = (bf16[512,1536]{1,0:T(8,128)(2,1)}, f32[512,1536]{1,0:T(8,128)S(1)}) fusion(f32[1536]{0:T(1024)S(1)} %copy-done.204, bf16[768,1536]{1,0:T(8,128)(2,1)S(1)} %copy-done, bf16[1,512,768]{2,1,0:T(8,128)(2,1)} %all_gather.51), kind=kOutput, calls=%fused_computation.51 | convolution fusion | flops 1259864064 | bytes 7870464 | tf_op jit(solution)/shard_map/bsd,df->bsf/dot_general | solution.py:43
  430.6 4.4 fusion.71
  435.1 5.4 fusion.184
  440.5 3.6 fusion.162
  444.1 3.6 fusion.202
  450.3 5.4 fusion.193
  455.7 3.5 fusion.173
  459.2 3.7 fusion.167
  465.3 9.8 %add_add_fusion.1 = f32[768,1536]{1,0:T(8,128)} fusion(f32[768,1536]{1,0:T(8,128)} %fusion.184, f32[768,1536]{1,0:T(8,128)} %fusion.202, f32[768,1536]{1,0:T(8,128)} %fusion.193, bf16[512,1536]{1,0:T(8,128)(2,1)} %copy-done.129, bf16[1,512,768]{2,1,0:T(8,128)(2,1)} %copy-done.95), kind=kOutput, calls=%fused_computation.33 | convolution fusion | flops 1211498496 | bytes 21233664 | tf_op jit(solution)/shard_map/bsd,bsf->df/dot_general | solution.py:43
  475.2 9.2 add_add_fusion
  484.4 3.8 multiply_reduce_fusion.7
  490.0 20.2 %reduce-scatter.19.cloned.1.call-done = bf16[1,256,768]{2,1,0:T(8,128)(2,1)} async-done(((bf16[1,512,768]{2,1,0:T(8,128)(2,1)}), bf16[1,256,768]{2,1,0:T(8,128)(2,1)}) %reduce-scatter.19.cloned.1.call-update) | async-done | bytes 393232 | tf_op jit(solution)/shard_map/reduce_scatter | solution.py:136
  510.2 4.9 fusion.215
  515.2 19.0 %all_gather.63 = bf16[1,512,768]{2,1,0:T(8,128)(2,1)S(1)} all-gather(bf16[1,256,768]{2,1,0:T(8,128)(2,1)S(1)} %convert_element_type.637), channel_id=1, replica_groups=mesh['dp'=16,'mp'=2] {'mp'}, dimensions={1}, use_global_device_ids=true | all-gather | bytes 1179648 | tf_op jit(solution)/shard_map/all_gather | solution.py:159
  545.9 3.2 fusion.214
  549.2 8.5 all_gather.59
  558.2 4.6 multiply_reduce_fusion.2
  569.1 8.7 all_gather.57
  610.7 3.7 fusion.72
  646.3 3.0 reduce-scatter.35.cloned.1.call-done
  649.3 3.4 fusion.155
  655.3 8.4 all-reduce.2
  663.6 64.5 %all-reduce = (f32[768]{0:T(1024)}, f32[768]{0:T(1024)}, f32[384]{0:T(512)}, f32[384]{0:T(512)}, f32[768]{0:T(1024)}, /*index=5*/f32[768]{0:T(1024)}, f32[768]{0:T(1024)}, f32[1536]{0:T(1024)}, f32[768]{0:T(1024)}) all-reduce(f32[768]{0:T(1024)} %get-tuple-element.79, ...), channel_id=1, replica_groups=mesh['dp'=16,'mp'=2] {'dp'}, use_global_device_ids=true, to_apply=%region_65.66 | all-reduce | flops 6912 | bytes 55296 | tf_op jit(solution)/shard_map/psum | solution.py:17
  738.0 178.4 %all-reduce.5.cloned.1.call-done = (f32[768,384]{1,0:T(8,128)}, f32[768,384]{1,0:T(8,128)}, f32[768,384]{1,0:T(8,128)}, f32[384,768]{1,0:T(8,128)}, f32[768,1536]{1,0:T(8,128)}, /*index=5*/f32[1536,768]{1,0:T(8,128)}) async-done(((f32[768,384]{1,0:T(8,128)}, f32[768,384]{1,0:T(8,128)}, f32[768,384]{1,0:T(8,128)}, f32[384,768]{1,0:T(8,128)}, f32[768,1536]{1,0:T(8,128)}, /*index=5*/f32[1536,768]{1,0:T(8,128)}), ...) | async-done | bytes 14155792 | tf_op jit(solution)/shard_map/psum | solution.py:202
  (660 shorter events, 226.6 us)
Async XLA Ops:
  7.2 76.9 %copy-start = (bf16[768,1536]{1,0:T(8,128)(2,1)S(1)}, bf16[768,1536]{1,0:T(8,128)(2,1)}, u32[]{:S(2)}) copy-start(bf16[768,1536]{1,0:T(8,128)(2,1)} %param.32) | copy-start | bytes 7077892
  7.2 17.7 %copy-start.193 = (s32[4]{0:T(128)S(1)}, s32[4]{0:T(128)}, u32[]{:S(2)}) copy-start(s32[4]{0:T(128)} %param.19) | copy-start | bytes 52
  7.2 19.1 %copy-start.37 = (bf16[768,384]{1,0:T(8,128)(2,1)S(1)}, bf16[768,384]{1,0:T(8,128)(2,1)}, u32[]{:S(2)}) copy-start(bf16[768,384]{1,0:T(8,128)(2,1)} %param.25) | copy-start | bytes 1769476
  7.2 19.6 %copy-start.34 = (bf16[768,384]{1,0:T(8,128)(2,1)S(1)}, bf16[768,384]{1,0:T(8,128)(2,1)}, u32[]{:S(2)}) copy-start(bf16[768,384]{1,0:T(8,128)(2,1)} %param.23) | copy-start | bytes 1769476
  7.2 19.6 %copy-start.205 = (f32[384]{0:T(512)S(1)}, f32[384]{0:T(512)}, u32[]{:S(2)}) copy-start(f32[384]{0:T(512)} %param.24) | copy-start | bytes 4612
  7.2 62.2 %reduce-scatter.25.cloned.1.call-start = ((), (), s32[]{:S(2)}) async-start(), calls=%async_computation.20 | async-start | bytes 2359296 | tf_op jit(solution)/shard_map/reduce_scatter | solution.py:128
  8.6 18.8 %copy-start.158 = (f32[256]{0:T(256)}, f32[256]{0:T(256)S(1)}, u32[]{:S(2)}) copy-start(f32[256]{0:T(256)S(1)} %broadcast_multiply_fusion.19) | copy-start | bytes 3076
  10.9 18.1 %copy-start.175 = (f32[256]{0:T(256)}, f32[256]{0:T(256)S(1)}, u32[]{:S(2)}) copy-start(f32[256]{0:T(256)S(1)} %add_rsqrt_fusion.3) | copy-start | bytes 3076
  37.9 90.4 %reduce-scatter.41.cloned.1.call-start = ((), (), s32[]{:S(2)}) async-start(), calls=%async_computation.28 | async-start | bytes 2359296 | tf_op jit(solution)/shard_map/reduce_scatter | solution.py:152
  101.0 47.7 %reduce-scatter.27.cloned.1.call-start = ((), (), s32[]{:S(2)}) async-start(), calls=%async_computation.21 | async-start | bytes 1179648 | tf_op jit(solution)/shard_map/reduce_scatter | solution.py:136
  105.5 91.1 %reduce-scatter.43.cloned.1.call-start = ((), (), s32[]{:S(2)}) async-start(), calls=%async_computation.29 | async-start | bytes 1179648 | tf_op jit(solution)/shard_map/reduce_scatter | solution.py:195
  177.5 19.1 %copy-start.144 = (f32[768]{0:T(1024)S(1)}, f32[768]{0:T(1024)}, u32[]{:S(2)}) copy-start(f32[768]{0:T(1024)} %param.21) | copy-start | bytes 9220
  179.0 149.3 %reduce-scatter.17.cloned.1.call-start = ((), (), s32[]{:S(2)}) async-start(), calls=%async_computation.16 | async-start | bytes 2359296 | tf_op jit(solution)/shard_map/reduce_scatter | solution.py:128
  180.4 35.2 %copy-start.148 = (f32[256]{0:T(256)}, f32[256]{0:T(256)S(1)}, u32[]{:S(2)}) copy-start(f32[256]{0:T(256)S(1)} %broadcast_multiply_fusion.17) | copy-start | bytes 3076
  181.1 34.5 %copy-start.156 = (f32[256]{0:T(256)}, f32[256]{0:T(256)S(1)}, u32[]{:S(2)}) copy-start(f32[256]{0:T(256)S(1)} %get-tuple-element.187) | copy-start | bytes 3076
  181.1 34.5 %copy-start.157 = (f32[256]{0:T(256)}, f32[256]{0:T(256)S(1)}, u32[]{:S(2)}) copy-start(f32[256]{0:T(256)S(1)} %get-tuple-element.188) | copy-start | bytes 3076
  199.5 16.7 %copy-start.176 = (f32[256]{0:T(256)}, f32[256]{0:T(256)S(1)}, u32[]{:S(2)}) copy-start(f32[256]{0:T(256)S(1)} %add_rsqrt_fusion.7) | copy-start | bytes 3076
  199.5 16.7 %copy-start.177 = (f32[256]{0:T(256)}, f32[256]{0:T(256)S(1)}, u32[]{:S(2)}) copy-start(f32[256]{0:T(256)S(1)} %add_rsqrt_fusion.5) | copy-start | bytes 3076
  199.6 16.6 %copy-start.178 = (f32[256]{0:T(256)}, f32[256]{0:T(256)S(1)}, u32[]{:S(2)}) copy-start(f32[256]{0:T(256)S(1)} %add_rsqrt_fusion.1) | copy-start | bytes 3076
  225.5 21.0 %copy-start.207 = (f32[384]{0:T(512)S(1)}, f32[384]{0:T(512)}, u32[]{:S(2)}) copy-start(f32[384]{0:T(512)} %param.24) | copy-start | bytes 4612
  227.2 101.1 %reduce-scatter.21.cloned.1.call-start = ((), (), s32[]{:S(2)}) async-start(), calls=%async_computation.18 | async-start | bytes 2359296 | tf_op jit(solution)/shard_map/reduce_scatter | solution.py:128
  227.9 23.8 %copy-start.187 = (pred[512]{0:T(512)(128)(4,1)}, pred[512]{0:T(512)(128)(4,1)S(1)}, u32[]{:S(2)}) copy-start(pred[512]{0:T(512)(128)(4,1)S(1)} %iota_compare_fusion.2) | copy-start | bytes 1540
  258.6 70.1 %reduce-scatter.29.cloned.1.call-start = ((), (), s32[]{:S(2)}) async-start(), calls=%async_computation.22 | async-start | bytes 2359296 | tf_op jit(solution)/shard_map/reduce_scatter | solution.py:128
  259.2 16.5 %copy-start.189 = (pred[512]{0:T(512)(128)(4,1)}, pred[512]{0:T(512)(128)(4,1)S(1)}, u32[]{:S(2)}) copy-start(pred[512]{0:T(512)(128)(4,1)S(1)} %iota_compare_fusion) | copy-start | bytes 1540
  280.8 31.6 %copy-start.121 = (bf16[1,256,768]{2,1,0:T(8,128)(2,1)S(1)}, bf16[1,256,768]{2,1,0:T(8,128)(2,1)}, u32[]{:S(2)}) copy-start(bf16[1,256,768]{2,1,0:T(8,128)(2,1)} %get-tuple-element.117) | copy-start | bytes 1179652
  282.6 46.1 %copy-start.174 = (f32[768]{0:T(1024)S(1)}, f32[768]{0:T(1024)}, u32[]{:S(2)}) copy-start(f32[768]{0:T(1024)} %param.29) | copy-start | bytes 9220
  282.6 201.7 %reduce-scatter.33.cloned.1.call-start = ((), (), s32[]{:S(2)}) async-start(), calls=%async_computation.24 | async-start | bytes 2359296 | tf_op jit(solution)/shard_map/reduce_scatter | solution.py:152
  361.8 122.5 %reduce-scatter.45.cloned.1.call-start = ((), (), s32[]{:S(2)}) async-start(), calls=%async_computation.30 | async-start | bytes 2359296 | tf_op jit(solution)/shard_map/reduce_scatter | solution.py:152
  377.6 29.4 %copy-start.95 = (bf16[1,512,768]{2,1,0:T(8,128)(2,1)}, bf16[1,512,768]{2,1,0:T(8,128)(2,1)S(1)}, u32[]{:S(2)}) copy-start(bf16[1,512,768]{2,1,0:T(8,128)(2,1)S(1)} %all_gather.55) | copy-start | bytes 2359300
  413.6 70.8 %reduce-scatter.37.cloned.1.call-start = ((), (), s32[]{:S(2)}) async-start(), calls=%async_computation.26 | async-start | bytes 2359296 | tf_op jit(solution)/shard_map/reduce_scatter | solution.py:152
  430.5 59.5 %reduce-scatter.31.cloned.1.call-start = ((), (), s32[]{:S(2)}) async-start(), calls=%async_computation.23 | async-start | bytes 1179648 | tf_op jit(solution)/shard_map/reduce_scatter | solution.py:136
  435.0 75.2 %reduce-scatter.19.cloned.1.call-start = ((), (), s32[]{:S(2)}) async-start(), calls=%async_computation.17 | async-start | bytes 1179648 | tf_op jit(solution)/shard_map/reduce_scatter | solution.py:136
  450.0 95.9 %reduce-scatter.23.cloned.1.call-start = ((), (), s32[]{:S(2)}) async-start(), calls=%async_computation.19 | async-start | bytes 1179648 | tf_op jit(solution)/shard_map/reduce_scatter | solution.py:136
  465.2 181.1 %reduce-scatter.47.cloned.1.call-start = ((), (), s32[]{:S(2)}) async-start(), calls=%async_computation.31 | async-start | bytes 1179648 | tf_op jit(solution)/shard_map/reduce_scatter | solution.py:195
  484.3 25.9 %copy-start.146 = (f32[768]{0:T(1024)S(1)}, f32[768]{0:T(1024)}, u32[]{:S(2)}) copy-start(f32[768]{0:T(1024)} %param.35) | copy-start | bytes 9220
  510.2 24.0 %copy-start.32 = (bf16[384,768]{1,0:T(8,128)(2,1)S(1)}, bf16[384,768]{1,0:T(8,128)(2,1)}, u32[]{:S(2)}) copy-start(bf16[384,768]{1,0:T(8,128)(2,1)} %param.28) | copy-start | bytes 1769476
  510.2 26.2 %slice-start.4 = ((s8[6291456]{0:T(1024)(128)(4,1)}), s8[4194304]{0:T(1024)(128)(4,1)S(1)}, s32[]{:S(2)}) async-start(s8[6291456]{0:T(1024)(128)(4,1)} %bitcast.416), calls=%async_computation.37 | async-start | bytes 8388608
  515.2 21.3 %copy-start.48 = (f32[1,256,768]{2,1,0:T(8,128)}, f32[1,256,768]{2,1,0:T(8,128)S(1)}, u32[]{:S(2)}) copy-start(f32[1,256,768]{2,1,0:T(8,128)S(1)} %get-tuple-element.109) | copy-start | bytes 2359300
  515.2 19.6 %copy-start.11 = (bf16[6,512,512]{1,2,0:T(8,128)(2,1)S(1)}, bf16[6,512,512]{1,2,0:T(8,128)(2,1)}, u32[]{:S(2)}) copy-start(bf16[6,512,512]{1,2,0:T(8,128)(2,1)} %copy-done.10) | copy-start | bytes 9437188
  515.2 21.3 %slice-start.5 = ((s8[6291456]{0:T(1024)(128)(4,1)}), s8[2097152]{0:T(1024)(128)(4,1)S(1)}, s32[]{:S(2)}) async-start(s8[6291456]{0:T(1024)(128)(4,1)} %bitcast.416), calls=%async_computation.38 | async-start | bytes 4194304
  536.5 54.4 %copy-start.57 = (bf16[6,64,512]{2,1,0:T(8,128)(2,1)}, bf16[6,64,512]{2,1,0:T(8,128)(2,1)S(1)}, u32[]{:S(2)}) copy-start(bf16[6,64,512]{2,1,0:T(8,128)(2,1)S(1)} %get-tuple-element.172) | copy-start | bytes 1179652
  592.5 53.8 %reduce-scatter.39.cloned.1.call-start = ((), (), s32[]{:S(2)}) async-start(), calls=%async_computation.27 | async-start | bytes 1179648 | tf_op jit(solution)/shard_map/reduce_scatter | solution.py:195
  610.7 38.6 %reduce-scatter.35.cloned.1.call-start = ((), (), s32[]{:S(2)}) async-start(), calls=%async_computation.25 | async-start | bytes 1179648 | tf_op jit(solution)/shard_map/reduce_scatter | solution.py:195
  624.0 292.5 %all-reduce.5.cloned.1.call-start = ((), (), s32[]{:S(2)}) async-start(), calls=%async_computation.32 | async-start | bytes 28311552 | tf_op jit(solution)/shard_map/psum | solution.py:202
  631.2 18.1 %copy-start.145 = (f32[768]{0:T(1024)S(1)}, f32[768]{0:T(1024)}, u32[]{:S(2)}) copy-start(f32[768]{0:T(1024)} %param.21) | copy-start | bytes 9220
  631.2 18.1 %copy-start.149 = (f32[256]{0:T(256)S(1)}, f32[256]{0:T(256)}, u32[]{:S(2)}) copy-start(f32[256]{0:T(256)} %copy-done.148) | copy-start | bytes 3076
  631.2 101.3 %copy-start.43 = (f32[1,256,768]{2,1,0:T(8,128)S(1)}, f32[1,256,768]{2,1,0:T(8,128)}, u32[]{:S(2)}) copy-start(f32[1,256,768]{2,1,0:T(8,128)} %copy-done.42) | copy-start | bytes 2359300
  646.3 88.5 %copy-start.122 = (bf16[1,256,768]{2,1,0:T(8,128)(2,1)S(1)}, bf16[1,256,768]{2,1,0:T(8,128)(2,1)}, u32[]{:S(2)}) copy-start(bf16[1,256,768]{2,1,0:T(8,128)(2,1)} %reduce-scatter.39.cloned.1.call-done) | copy-start | bytes 1179652
  (190 other events, 890.7 us)
Sparse Core Ops, SparseCore 0:
  38.1 31.3 reduce-scatter.24
  101.1 27.2 reduce-scatter.40
  131.2 17.4 reduce-scatter.26
  179.2 17.4 reduce-scatter.42
  227.3 29.6 reduce-scatter.16
  259.8 28.8 reduce-scatter.20
  291.0 37.6 reduce-scatter.28
  361.9 37.5 reduce-scatter.32
  413.7 27.7 reduce-scatter.44
  443.6 26.0 reduce-scatter.36
  472.5 17.4 reduce-scatter.30
  492.8 17.4 reduce-scatter.18
  513.0 23.4 reduce-scatter.22
  592.6 17.4 reduce-scatter.46
  612.2 17.4 reduce-scatter.38
  631.9 17.4 reduce-scatter.34
  655.4 260.9 all-reduce.4
